TPU v7x, 32 devices: a whole 2x2x4 slice. The times are simulated.
32 devices in a mesh: row: 8 (over y, x, core), ck: 4 (over z).
Axes of the slice: x: 2, y: 2, z: 4, core: 2. Of those that a mesh axis runs over, the one named last changes fastest.
Arguments:
- amp_tiles: bfloat16 [8, 4, 8, 16, 128, 128], P('row', 'ck'), may hold values from -6 to 6
- tile_pos: int32 [8, 4, 8, 16], P(None, 'ck'), may hold values from 0 to 2303, as said below
- tile_count: int32 [8, 4, 8], P(None, 'ck'), may hold values from 0 to 16, as said below
- cycle_integrals: bfloat16 [147456, 512], P('ck'), may hold values from -0.09375 to 0.09375
- row_gap: float32 [8192], P(('row', 'ck')), may hold values from 0.5 to 4
- col_gap: float32 [512], replicated, may hold values from 0.5 to 4
Outputs:
- new_amp: bfloat16 [8192, 512], P(('row', 'ck'))
Inputs may be any that keep to these rules, and one draw needn't show every extreme that they name: `tile_pos`: slots 0 to tile_count - 1 of each list are live, the others hold no tile. Within one ck group and one row owner all slots' positions are distinct. `tile_count`: in every ck group one row owner receives 16 live tiles from every storage owner.
All inputs are finite; a program needn't handle non-finite values.
Results may differ from a plain program's by a relative error of at most 0.001.
Values may be sent and summed in bfloat16 or wider, within the bound.
No kernel may reach another device: no remote copies, remote signals or barrier semaphores. Data moves between devices by JAX's collectives and lax.ppermute only.
A program may use at most 320 MiB of HBM per device.

v0:
```python
import jax
import jax.numpy as jnp
from jax import lax
from jax.sharding import PartitionSpec as P

TILE = 128
KT_DEV = 288
CAP = 16


def slot_products(amp_slots, positions, integrals):
    tile_width = amp_slots.shape[-1]
    blocks = integrals.reshape(-1, tile_width, integrals.shape[-1])
    picked = blocks[positions % blocks.shape[0]]
    return jnp.einsum("mrk,mkc->mrc", amp_slots, picked, preferred_element_type=jnp.float32)


def row_terms(products, tile_ids, live_mask, row_count):
    tile_width = products.shape[1]
    segment_total = row_count // tile_width
    inside = live_mask & (tile_ids >= 0) & (tile_ids < segment_total)
    target = jnp.where(inside, tile_ids, segment_total)
    summed = jax.ops.segment_sum(products, target, num_segments=segment_total + 1)[:segment_total]
    return summed.reshape(row_count, products.shape[2])


def on_device(amp_tiles, tile_pos, tile_count, cycle_integrals, row_gap, col_gap):
    my_row = lax.axis_index("row")
    slot_range = jnp.arange(CAP)
    share_rows = row_gap.shape[0]
    received = lax.all_to_all(amp_tiles, "row", split_axis=2, concat_axis=0, tiled=True)
    amp_slots = received.reshape(-1, TILE, TILE)
    positions = lax.dynamic_index_in_dim(tile_pos, my_row, 2, keepdims=False).reshape(-1)
    counts = lax.dynamic_index_in_dim(tile_count, my_row, 2, keepdims=False).reshape(-1)
    live_mask = (slot_range[None, :] < counts[:, None]).reshape(-1)
    tile_ids = positions // KT_DEV
    products = slot_products(amp_slots, positions, cycle_integrals)
    reduced = lax.psum_scatter(
        row_terms(products, tile_ids, live_mask, lax.axis_size("ck") * share_rows),
        "ck",
        scatter_dimension=0,
        tiled=True,
    )
    quotient = (reduced / (row_gap[:, None] + col_gap[None, :])).astype(jnp.bfloat16)
    return lax.all_to_all(quotient, "row", split_axis=0, concat_axis=0, tiled=True)


def solution(mesh):
    return jax.shard_map(
        on_device,
        mesh=mesh,
        in_specs=(
            P("row", "ck", None, None, None, None),
            P(None, "ck", None, None),
            P(None, "ck", None),
            P("ck", None),
            P(("row", "ck")),
            P(),
        ),
        out_specs=P(("row", "ck"), None),
        check_vma=False,
    )
```

profile of v0, /device:TPU:0, one launch (start us, length us, event | category | flops | bytes accessed | tf_op | source)
XLA Modules:
  0.0 227.3 jit_solution(11846260106764262696)
XLA Ops:
  6.5 0.0 copy-start
  6.5 5.3 %all-to-all-start = ((bf16[1,1,8,16,128,128]{5,4,3,1,0,2:T(8,128)(2,1)}), bf16[1,1,8,16,128,128]{5,4,3,1,0,2:T(8,128)(2,1)}, u32[]{:S(2)}, u32[]{:S(2)}) async-start(bf16[1,1,8,16,128,128]{5,4,3,1,0,2:T(8,128)(2,1)} %bitcast.16), calls=%async_computation | async-start | bytes 8388608 | tf_op jit(solution)/shard_map/all_to_all | solution.py:31
  11.9 0.0 reduce-scatter.2.cloned.1.call-start
  11.9 0.8 remainder_reduce_fusion
  12.7 0.1 div.20
  12.8 0.1 rem.30
  12.9 0.0 copy-done
  12.9 0.3 dynamic-slice_reduce_fusion
  13.2 0.1 iota_compare_fusion
  13.3 0.1 lt.66
  13.4 0.8 compare_reduce_fusion
  14.2 0.1 ne.52
  14.3 12.6 %gather_fusion = bf16[128,128,512]{2,1,0:T(8,128)(2,1)} fusion(bf16[288,128,512]{2,1,0:T(8,128)(2,1)} %bitcast.15, s32[1024]{0:T(1024)S(1)} %pad_clamp_fusion), kind=kCustom, calls=%fused_computation | custom fusion | bytes 33554944 | tf_op jit(solution)/shard_map/gather | solution.py:14
  26.9 34.2 %all-to-all-done = bf16[1,1,8,16,128,128]{5,4,3,1,0,2:T(8,128)(2,1)} async-done(((bf16[1,1,8,16,128,128]{5,4,3,1,0,2:T(8,128)(2,1)}), bf16[1,1,8,16,128,128]{5,4,3,1,0,2:T(8,128)(2,1)}, u32[]{:S(2)}, u32[]{:S(2)}) %all-to-all-start) | async-done | bytes 4194336 | tf_op jit(solution)/shard_map/all_to_all | solution.py:31
  61.1 22.3 %convolution_bitcast_fusion = f32[128,128,512]{1,2,0:T(8,128)} fusion(bf16[128,128,512]{2,1,0:T(8,128)(2,1)} %gather_fusion, bf16[128,128,128]{2,1,0:T(8,128)(2,1)} %bitcast.4), kind=kOutput, calls=%fused_computation.2 | convolution fusion | flops 2147483648 | bytes 54525952 | tf_op jit(solution)/shard_map/mrk,mkc->mrc/dot_general | solution.py:15
  83.4 33.4 %copy.12 = f32[128,128,512]{2,1,0:T(8,128)} copy(f32[128,128,512]{1,2,0:T(8,128)} %convolution_bitcast_fusion) | data formatting | bytes 67108864 | tf_op jit(solution)/shard_map/mrk,mkc->mrc/dot_general | solution.py:15
  116.8 0.3 broadcast_in_dim.3
  117.1 0.0 copy-start.2
  117.1 0.0 copy-start.3
  117.1 0.0 copy-start.1
  117.2 45.1 %scatter_fusion = f32[9,128,512]{2,1,0:T(8,128)S(1)} fusion(f32[9,128,512]{2,1,0:T(8,128)S(1)} %broadcast_in_dim.3, s32[128]{0:T(128)S(1)} %get-tuple-element.8, f32[128,128,512]{2,1,0:T(8,128)} %copy.12), kind=kCustom, calls=%fused_computation.1 | custom fusion | flops 8388608 | bytes 100663808 | tf_op jit(solution)/shard_map/scatter-add | solution.py:23
  162.3 1.6 slice.6
  163.9 0.0 reduce-scatter.2.cloned.1.call-update
  163.9 44.3 %reduce-scatter.2.cloned.1.call-done = f32[256,512]{1,0:T(8,128)} async-done(((f32[1024,512]{1,0:T(8,128)}), f32[256,512]{1,0:T(8,128)}) %reduce-scatter.2.cloned.1.call-update) | async-done | bytes 524304 | tf_op jit(solution)/shard_map/reduce_scatter | solution.py:38
  208.2 0.0 copy-done.2
  208.2 0.0 copy-done.3
  208.2 1.2 divide_convert_fusion
  209.4 10.4 %all_to_all.21 = bf16[8,32,512]{2,1,0:T(8,128)(2,1)S(1)} all-to-all(bf16[8,32,512]{2,1,0:T(8,128)(2,1)S(1)} %bitcast.17), channel_id=1, replica_groups=mesh['row'=8,'ck'=4] {'row'}, dimensions={0} | all-to-all | bytes 524288 | tf_op jit(solution)/shard_map/all_to_all | solution.py:45
  219.7 0.7 copy.16
  220.4 0.0 copy-done.1
  (2 shorter events, 0.0 us)
Async XLA Ops:
  6.5 6.4 %copy-start = (s32[8,1,8]{2,1,0:T(1,128)S(1)}, s32[8,1,8]{2,1,0:T(1,128)}, u32[]{:S(2)}) copy-start(s32[8,1,8]{2,1,0:T(1,128)} %param.8) | copy-start | bytes 772
  6.5 54.5 %all-to-all-start = ((bf16[1,1,8,16,128,128]{5,4,3,1,0,2:T(8,128)(2,1)}), bf16[1,1,8,16,128,128]{5,4,3,1,0,2:T(8,128)(2,1)}, u32[]{:S(2)}, u32[]{:S(2)}) async-start(bf16[1,1,8,16,128,128]{5,4,3,1,0,2:T(8,128)(2,1)} %bitcast.16), calls=%async_computation | async-start | bytes 8388608 | tf_op jit(solution)/shard_map/all_to_all | solution.py:31
  11.9 196.3 %reduce-scatter.2.cloned.1.call-start = ((), (), s32[]{:S(2)}) async-start(), calls=%async_computation.3 | async-start | bytes 2621440 | tf_op jit(solution)/shard_map/reduce_scatter | solution.py:38
  117.1 91.1 %copy-start.2 = (f32[512]{0:T(512)S(1)}, f32[512]{0:T(512)}, u32[]{:S(2)}) copy-start(f32[512]{0:T(512)} %param.11) | copy-start | bytes 6148
  117.1 91.1 %copy-start.3 = (f32[256]{0:T(256)S(1)}, f32[256]{0:T(256)}, u32[]{:S(2)}) copy-start(f32[256]{0:T(256)} %param.10) | copy-start | bytes 3076
  117.1 103.3 %copy-start.1 = (s32[8,1,8]{2,1,0:T(1,128)S(1)}, s32[8,1,8]{2,1,0:T(1,128)}, u32[]{:S(2)}) copy-start(s32[8,1,8]{2,1,0:T(1,128)} %param.8) | copy-start | bytes 772
Sparse Core Ops, SparseCore 0:
  164.0 44.0 reduce-scatter.1
where the time goes:
time: 229 us; the launch traced here: 227 us
  waiting for transfers between devices  78.5 us (34%)
  local copies, waits for them, and re-layouts  49.3 us (22%)
  other arithmetic  48 us (21%)
  matrix products  22.3 us (10%)
  between operations  13.5 us (6%)
  blocking collectives  10.4 us (5%)
  starting transfers between devices  5.37 us (2%)
    scatter-add x1, other arithmetic, row_terms(): jax.ops.segment_sum(products, target, num_segments=segment_total + 1)  45.1 us
    reduce_scatter x1, waiting for transfers between devices, on_device(): lax.psum_scatter(row_terms(products, tile_ids, live_mask, lax.axis_size('...  44.3 us
    all_to_all x1, waiting for transfers between devices, on_device(): lax.all_to_all(amp_tiles, 'row', split_axis=2, concat_axis=0, tiled=True)  34.2 us
    dot_general x1, local copies, waits for them, and re-layouts, slot_products(): jnp.einsum('mrk,mkc->mrc', amp_slots, picked, preferred_element_type=jnp....  33.4 us
    dot_general x1, matrix products, slot_products(): jnp.einsum('mrk,mkc->mrc', amp_slots, picked, preferred_element_type=jnp....  22.3 us
    gather x1, local copies, waits for them, and re-layouts, slot_products(): picked = blocks[positions % blocks.shape[0]]  12.6 us
    all_to_all x1, blocking collectives, on_device(): lax.all_to_all(quotient, 'row', split_axis=0, concat_axis=0, tiled=True)  10.4 us
    all_to_all x1, starting transfers between devices, on_device(): lax.all_to_all(amp_tiles, 'row', split_axis=2, concat_axis=0, tiled=True)  5.33 us
  transfers between devices with their start and end apart: 2, of which 2 were waited for; matrix products, arithmetic and copies ran while one was open for 7% of the time, Pallas kernels for 0%

commit v1 on v0

--- a/solution.py
+++ b/solution.py
@@ -28,7 +28,10 @@
     my_row = lax.axis_index("row")
     slot_range = jnp.arange(CAP)
     share_rows = row_gap.shape[0]
-    received = lax.all_to_all(amp_tiles, "row", split_axis=2, concat_axis=0, tiled=True)
+    received = jnp.concatenate(
+        lax.all_to_all(jnp.stack(jnp.split(amp_tiles, lax.axis_size("row"), axis=2)), "row", 0, 0),
+        axis=0,
+    )
     amp_slots = received.reshape(-1, TILE, TILE)
     positions = lax.dynamic_index_in_dim(tile_pos, my_row, 2, keepdims=False).reshape(-1)
     counts = lax.dynamic_index_in_dim(tile_count, my_row, 2, keepdims=False).reshape(-1)

time: 229 us -> 206 us (0.90)
  local copies, waits for them, and re-layouts: 49.3 us -> 31 us
  matrix products: 22.3 us -> 17.9 us
    dot_general x1 -> x0, local copies, waits for them, and re-layouts: 33.4 us -> none  [slot_products(): jnp.einsum('mrk,mkc->mrc', amp_slots, picked, preferred_element_type=jnp....]
    unnamed x9 -> x16, local copies, waits for them, and re-layouts: 0.73 us -> 14 us
    dot_general x1, matrix products: 22.3 us -> 17.9 us  [slot_products(): jnp.einsum('mrk,mkc->mrc', amp_slots, picked, preferred_element_type=jnp....]
where the time goes in v1:
time: 206 us; the launch traced here: 204 us
  waiting for transfers between devices  78.5 us (38%)
  other arithmetic  48 us (23%)
  local copies, waits for them, and re-layouts  31 us (15%)
  matrix products  17.9 us (9%)
  between operations  13.5 us (7%)
  blocking collectives  10.3 us (5%)
  starting transfers between devices  5.24 us (3%)
    scatter-add x1, other arithmetic, row_terms(): jax.ops.segment_sum(products, target, num_segments=segment_total + 1)  45.1 us
    reduce_scatter x1, waiting for transfers between devices, on_device(): lax.psum_scatter(row_terms(products, tile_ids, live_mask, lax.axis_size('...  44.3 us
    all_to_all x1, waiting for transfers between devices, on_device(): lax.all_to_all(jnp.stack(jnp.split(amp_tiles, lax.axis_size('row'), axis=...  34.2 us
    dot_general x1, matrix products, slot_products(): jnp.einsum('mrk,mkc->mrc', amp_slots, picked, preferred_element_type=jnp....  17.9 us
    unnamed x16, local copies, waits for them, and re-layouts  14 us
    gather x1, local copies, waits for them, and re-layouts, slot_products(): picked = blocks[positions % blocks.shape[0]]  12.6 us
    all_to_all x1, blocking collectives, on_device(): lax.all_to_all(quotient, 'row', split_axis=0, concat_axis=0, tiled=True)  10.3 us
    all_to_all x1, starting transfers between devices, on_device(): lax.all_to_all(jnp.stack(jnp.split(amp_tiles, lax.axis_size('row'), axis=...  5.2 us
  transfers between devices with their start and end apart: 2, of which 2 were waited for; matrix products, arithmetic and copies ran while one was open for 7% of the time, Pallas kernels for 0%

profile of v1, /device:TPU:0, one launch (start us, length us, event | category | flops | bytes accessed | tf_op | source)
XLA Modules:
  0.0 204.5 jit_solution(6590056450716323353)
XLA Ops:
  6.5 1.9 bitcast_dynamic-update-slice_fusion.7
  8.4 1.9 bitcast_dynamic-update-slice_fusion.6
  10.3 1.9 bitcast_dynamic-update-slice_fusion.5
  12.2 1.9 bitcast_dynamic-update-slice_fusion.4
  14.1 1.9 bitcast_dynamic-update-slice_fusion.3
  16.0 1.9 bitcast_dynamic-update-slice_fusion.2
  17.9 1.9 bitcast_dynamic-update-slice_fusion.1
  19.8 1.9 bitcast_dynamic-update-slice_fusion
  21.7 5.2 %all-to-all-start = ((bf16[8,1,1,1,16,128,128]{6,5,4,3,2,1,0:T(8,128)(2,1)}), bf16[8,1,1,1,16,128,128]{6,5,4,3,2,1,0:T(8,128)(2,1)}, u32[]{:S(2)}, u32[]{:S(2)}) async-start(bf16[8,1,1,1,16,128,128]{6,5,4,3,2,1,0:T(8,128)(2,1)} %bitcast_dynamic-update-slice_fusion), calls=%async_computation | async-start | bytes 8388608 | tf_op jit(solution)/shard_map/all_to_all | solution.py:32
  26.9 0.0 reduce-scatter.2.cloned.1.call-start
  27.0 0.8 remainder_reduce_fusion
  27.8 0.1 div.20
  27.9 0.1 rem.30
  27.9 0.3 dynamic-slice_reduce_fusion
  28.2 0.1 iota_compare_fusion
  28.3 0.1 lt.66
  28.4 0.8 compare_reduce_fusion
  29.2 0.1 ne.52
  29.3 12.6 %gather_fusion = bf16[128,128,512]{2,1,0:T(8,128)(2,1)} fusion(bf16[288,128,512]{2,1,0:T(8,128)(2,1)} %bitcast.28, s32[1024]{0:T(1024)S(1)} %pad_clamp_fusion), kind=kCustom, calls=%fused_computation | custom fusion | bytes 33554944 | tf_op jit(solution)/shard_map/gather | solution.py:14
  41.9 34.2 %all-to-all-done = bf16[8,1,1,1,16,128,128]{6,5,4,3,2,1,0:T(8,128)(2,1)} async-done(((bf16[8,1,1,1,16,128,128]{6,5,4,3,2,1,0:T(8,128)(2,1)}), bf16[8,1,1,1,16,128,128]{6,5,4,3,2,1,0:T(8,128)(2,1)}, u32[]{:S(2)}, u32[]{:S(2)}) %all-to-all-start) | async-done | bytes 4194336 | tf_op jit(solution)/shard_map/all_to_all | solution.py:32
  76.1 17.9 %fusion.2 = f32[128,128,512]{2,1,0:T(8,128)} fusion(bf16[128,128,128]{2,1,0:T(8,128)(2,1)} %bitcast.9, bf16[128,128,512]{2,1,0:T(8,128)(2,1)} %gather_fusion), kind=kOutput, calls=%fused_computation.24 | convolution fusion | flops 2147483648 | bytes 54525952 | tf_op jit(solution)/shard_map/mrk,mkc->mrc/dot_general | solution.py:15
  94.0 0.3 broadcast_in_dim.3
  94.3 0.0 copy-start.1
  94.3 45.1 %scatter_fusion = f32[9,128,512]{2,1,0:T(8,128)S(1)} fusion(f32[9,128,512]{2,1,0:T(8,128)S(1)} %broadcast_in_dim.3, s32[128]{0:T(128)S(1)} %get-tuple-element.8, f32[128,128,512]{2,1,0:T(8,128)} %fusion.2), kind=kCustom, calls=%fused_computation.1 | custom fusion | flops 8388608 | bytes 100663808 | tf_op jit(solution)/shard_map/scatter-add | solution.py:23
  139.4 0.0 copy-start.2
  139.4 0.0 copy-start.3
  139.4 1.6 slice.6
  141.1 0.0 reduce-scatter.2.cloned.1.call-update
  141.1 44.3 %reduce-scatter.2.cloned.1.call-done = f32[256,512]{1,0:T(8,128)} async-done(((f32[1024,512]{1,0:T(8,128)}), f32[256,512]{1,0:T(8,128)}) %reduce-scatter.2.cloned.1.call-update) | async-done | bytes 524304 | tf_op jit(solution)/shard_map/reduce_scatter | solution.py:41
  185.4 1.2 divide_convert_fusion
  186.6 10.3 %all_to_all.17 = bf16[8,32,512]{2,1,0:T(8,128)(2,1)S(1)} all-to-all(bf16[8,32,512]{2,1,0:T(8,128)(2,1)S(1)} %bitcast.29), channel_id=1, replica_groups=mesh['row'=8,'ck'=4] {'row'}, dimensions={0} | all-to-all | bytes 524288 | tf_op jit(solution)/shard_map/all_to_all | solution.py:48
  196.9 0.7 copy.16
  (7 shorter events, 0.0 us)
Async XLA Ops:
  6.5 21.4 %copy-start = (s32[8,1,8]{2,1,0:T(1,128)S(1)}, s32[8,1,8]{2,1,0:T(1,128)}, u32[]{:S(2)}) copy-start(s32[8,1,8]{2,1,0:T(1,128)} %param.8) | copy-start | bytes 772
  21.7 54.4 %all-to-all-start = ((bf16[8,1,1,1,16,128,128]{6,5,4,3,2,1,0:T(8,128)(2,1)}), bf16[8,1,1,1,16,128,128]{6,5,4,3,2,1,0:T(8,128)(2,1)}, u32[]{:S(2)}, u32[]{:S(2)}) async-start(bf16[8,1,1,1,16,128,128]{6,5,4,3,2,1,0:T(8,128)(2,1)} %bitcast_dynamic-update-slice_fusion), calls=%async_computation | async-start | bytes 8388608 | tf_op jit(solution)/shard_map/all_to_all | solution.py:32
  26.9 158.5 %reduce-scatter.2.cloned.1.call-start = ((), (), s32[]{:S(2)}) async-start(), calls=%async_computation.3 | async-start | bytes 2621440 | tf_op jit(solution)/shard_map/reduce_scatter | solution.py:41
  94.3 103.3 %copy-start.1 = (s32[8,1,8]{2,1,0:T(1,128)S(1)}, s32[8,1,8]{2,1,0:T(1,128)}, u32[]{:S(2)}) copy-start(s32[8,1,8]{2,1,0:T(1,128)} %param.8) | copy-start | bytes 772
  139.4 46.0 %copy-start.2 = (f32[512]{0:T(512)S(1)}, f32[512]{0:T(512)}, u32[]{:S(2)}) copy-start(f32[512]{0:T(512)} %param.11) | copy-start | bytes 6148
  139.4 45.9 %copy-start.3 = (f32[256]{0:T(256)S(1)}, f32[256]{0:T(256)}, u32[]{:S(2)}) copy-start(f32[256]{0:T(256)} %param.10) | copy-start | bytes 3076
Sparse Core Ops, SparseCore 0:
  141.2 44.0 reduce-scatter.1
